TPU v7x, 128 devices: a whole 4x4x4 slice. The times are simulated.
128 devices in a mesh: grp: 4 (over z), slab: 32 (over x, y, core).
Axes of the slice: x: 4, y: 4, z: 4, core: 2. Of those that a mesh axis runs over, the one named last changes fastest.
Arguments:
- probes: float32 [64, 512, 8, 512], P(None, 'slab', None, 'grp'), may hold values from -6 to 6
- courant: float32 [512, 8, 512], P('slab', None, 'grp'), may hold values from 0.02 to 0.18
- rec_cell: int32 [8192], P(('grp', 'slab')), may hold values from 0 to 16383
- rec_owner: int32 [8192, 1], P(('grp', 'slab')), may hold values from 0 to 31; in each aligned block of 64 rows (0 to 63, 64 to 127, ...) at most 8 rows name the same one
- trace_weight: float32 [8192], P(('grp', 'slab')), may hold values from 1 to 10
Outputs:
- wavefield: float32 [64, 512, 8, 512], P(None, 'slab', None, 'grp')
- q_basis: float32 [32768, 256], P(('grp', 'slab'))
- r_factor: float32 [64, 64], replicated
Inputs may be any that keep to these rules, and one draw needn't show every extreme that they name: `rec_owner`: among the receivers of one device no owner is named by more than 8; in every draw some device names some owner exactly 8 times.
All inputs are finite; a program needn't handle non-finite values.
Results may differ from a plain program's by a relative error of at most 0.00016.
Values sent between devices are 32-bit elements; how exact they have to be, the bound alone decides.
A program may use at most 192 MiB of HBM per device.

v0:
```python
import math
import jax
import jax.numpy as jnp
from jax import lax
from jax.sharding import PartitionSpec as P

PROBES = 64
CX = 16
CY = 8
CZ = 128
STEPS = 4
stencil_weights = (-205.0 / 72.0, 8.0 / 5.0, -1.0 / 5.0, 8.0 / 315.0, -1.0 / 560.0)


def with_halo(block, sides, width):
    for axis, dim in sides:
        count = lax.axis_size(axis)
        forward = [(i, i + 1) for i in range(count - 1)]
        backward = [(target, source) for source, target in forward]
        low = lax.ppermute(
            lax.slice_in_dim(block, block.shape[dim] - width, None, axis=dim), axis, forward
        )
        high = lax.ppermute(lax.slice_in_dim(block, 0, width, axis=dim), axis, backward)
        block = jnp.concatenate([low, block, high], axis=dim)
    return block


def laplace(padded):
    size_x = padded.shape[1] - 8
    size_y = padded.shape[2] - 8
    size_z = padded.shape[3] - 8
    center = padded[:, 4 : 4 + size_x, 4 : 4 + size_y, 4 : 4 + size_z]
    total = 3.0 * stencil_weights[0] * center
    for offset in range(1, 5):
        beside_all = padded[:, 4 + offset : 4 + offset + size_x, 4 : 4 + size_y, 4 : 4 + size_z]
        beside_all = (
            beside_all + padded[:, 4 - offset : 4 - offset + size_x, 4 : 4 + size_y, 4 : 4 + size_z]
        )
        beside_all = (
            beside_all + padded[:, 4 : 4 + size_x, 4 + offset : 4 + offset + size_y, 4 : 4 + size_z]
        )
        beside_all = (
            beside_all + padded[:, 4 : 4 + size_x, 4 - offset : 4 - offset + size_y, 4 : 4 + size_z]
        )
        beside_all = (
            beside_all + padded[:, 4 : 4 + size_x, 4 : 4 + size_y, 4 + offset : 4 + offset + size_z]
        )
        beside_all = (
            beside_all + padded[:, 4 : 4 + size_x, 4 : 4 + size_y, 4 - offset : 4 - offset + size_z]
        )
        total = total + stencil_weights[offset] * beside_all
    return total


def pad_middle(field):
    return jnp.pad(field, ((0, 0), (0, 0), (4, 4), (0, 0)))


def per_device(probes, courant, rec_cell, rec_owner, trace_weight):
    n_slab = lax.axis_size("slab")
    n_group = lax.axis_size("grp")
    rec_count = rec_cell.shape[0]
    capacity = max(2, 4 * rec_count // n_slab)
    cells = CX * CY * CZ
    picker = (jnp.arange(cells, dtype=jnp.int32)[:, None] == rec_cell[None, :]).astype(jnp.float32)
    speed = courant[None]
    previous = probes
    current = probes
    samples = []
    for moment in range(STEPS):
        extended = with_halo(current, (("grp", 3), ("slab", 1)), 4)
        advanced = 2.0 * current - previous + speed * laplace(pad_middle(extended))
        previous = current
        current = advanced
        samples.append(
            jnp.dot(
                current.reshape(PROBES, cells),
                picker,
                preferred_element_type=jnp.float32,
                precision=lax.Precision.HIGHEST,
            )
        )
    traces = jnp.stack(samples)
    rows = jnp.transpose(traces, (2, 0, 1)) * trace_weight[:, None, None]
    rows = rows.reshape(rec_count, STEPS * PROBES)
    sketch = rows.reshape(rec_count * STEPS, PROBES)
    gram = jnp.dot(
        sketch.T, sketch, preferred_element_type=jnp.float32, precision=lax.Precision.HIGHEST
    )
    owners = rec_owner[:, 0]
    hits = (owners[:, None] == jnp.arange(n_slab, dtype=jnp.int32)[None, :]).astype(jnp.int32)
    before = jnp.cumsum(hits, axis=0) - hits
    slots = jnp.sum(before * hits, axis=1)
    target = owners * capacity + slots
    placer = (target[:, None] == jnp.arange(n_slab * capacity, dtype=jnp.int32)[None, :]).astype(
        jnp.float32
    )
    outgoing = jnp.dot(
        placer.T, rows, preferred_element_type=jnp.float32, precision=lax.Precision.HIGHEST
    )
    incoming = lax.all_to_all(
        outgoing.reshape(n_slab, capacity, STEPS * PROBES),
        "slab",
        split_axis=0,
        concat_axis=0,
        tiled=True,
    )
    incoming = incoming.reshape(n_slab * capacity, STEPS * PROBES)
    lower = jnp.linalg.cholesky(lax.psum(gram, ("grp", "slab")))
    row_count = rec_count * n_slab * n_group * STEPS
    r_factor = lower.T / math.sqrt(row_count)
    solved = jax.scipy.linalg.solve_triangular(
        lower, incoming.reshape(n_slab * capacity * STEPS, PROBES).T, lower=True
    )
    q_basis = (solved.T * math.sqrt(row_count)).reshape(n_slab * capacity, STEPS * PROBES)
    return (current, q_basis, r_factor)


def solution(mesh):
    return jax.shard_map(
        per_device,
        mesh=mesh,
        in_specs=(
            P(None, "slab", None, "grp"),
            P("slab", None, "grp"),
            P(("grp", "slab")),
            P(("grp", "slab"), None),
            P(("grp", "slab")),
        ),
        out_specs=(P(None, "slab", None, "grp"), P(("grp", "slab"), None), P()),
        check_vma=False,
    )
```

profile of v0, /device:TPU:1, one launch (start us, length us, event | category | flops | bytes accessed | tf_op | source)
XLA Modules:
  0.0 824.6 jit_solution(537160318076101467)
XLA Ops:
  0.6 8.2 fusion.137
  8.8 3.7 copy.123
  13.8 3.7 copy.122
  17.5 5.0 collective-permute-start
  22.9 4.6 copy.90
  27.5 4.5 copy.89
  32.0 4.7 pad_maximum_fusion.21
  36.7 4.8 collective-permute-start.3
  41.5 2.1 collective-permute-start.2
  43.6 20.9 %collective-permute-done.3 = f32[64,4,8,136]{3,2,1,0:T(8,128)S(1)} collective-permute-done((f32[64,4,8,136]{3,2,1,0:T(8,128)S(1)}, f32[64,4,8,136]{3,2,1,0:T(8,128)S(1)}, u32[]{:S(2)}, u32[]{:S(2)}) %collective-permute-start.3) | collective-permute-done | bytes 1114144 | tf_op jit(solution)/shard_map/ppermute | solution.py:20
  64.5 4.4 collective-permute-done.2
  68.9 11.0 %pad_maximum_fusion = (f32[64,20,8,136]{3,2,1,0:T(8,128)}, f32[64,20,8,136]{3,2,1,0:T(8,128)}) fusion(f32[64,4,8,136]{3,2,1,0:T(8,128)S(1)} %collective-permute-done.2, f32[64,16,8,4]{3,2,1,0:T(8,128)S(1)} %copy-done.8, f32[64,16,8,128]{3,2,1,0:T(8,128)S(1)} %copy-done.5, f32[64,16,8,4]{3,2,1,0:T(8,128)S(1)} %copy-done.11, ...), kind=kLoop, calls=%fused_computation.67 | loop fusion | flops 8355840 | bytes 17825792 | tf_op jit(solution)/shard_map/concatenate | solution.py:24
  79.9 12.4 %select_maximum_fusion.12 = f32[64,24,16,136]{3,2,1,0:T(8,128)} fusion(f32[64,4,8,136]{3,2,1,0:T(8,128)S(1)} %collective-permute-done.2, f32[64,4,8,136]{3,2,1,0:T(8,128)S(1)} %collective-permute-done.3, f32[64,16,8,4]{3,2,1,0:T(8,128)S(1)} %copy-done.8, f32[64,16,8,128]{3,2,1,0:T(8,128)S(1)} %copy-done.5, f32[64,16,8,4]{3,2,1,0:T(8,128)S(1)} %copy-done.11), kind=kLoop, calls=%fused_computation.14 | loop fusion | flops 40108032 | bytes 20054016 | tf_op jit(solution)/shard_map/concatenate | solution.py:24
  92.3 88.4 %fusion.1 = f32[64,16,8,128]{3,2,1,0:T(8,128)} fusion(f32[64,16,8,128]{3,2,1,0:T(8,128)} %param.5, f32[64,16,8,4]{3,2,1,0:T(8,128)} %copy.89, f32[64,16,8,4]{3,2,1,0:T(8,128)} %copy.90, f32[64,24,16,136]{3,2,1,0:T(8,128)} %select_maximum_fusion.12, f32[64,20,8,136]{3,2,1,0:T(8,128)} %get-tuple-element.34, f32[64,20,8,136]{3,2,1,0:T(8,128)} %get-tuple-element.33, ...), kind=kLoop, calls=%fused_computation.76 | loop fusion | flops 42991616 | bytes 75825152 | tf_op jit(solution)/shard_map/add | solution.py:72
  180.7 8.2 fusion.136
  188.9 3.7 copy.94
  193.9 3.7 copy.93
  197.6 4.7 collective-permute-start.4
  202.4 4.6 copy.96
  207.0 4.5 copy.95
  211.5 4.7 pad_maximum_fusion.18
  216.1 3.4 collective-permute-start.7
  219.6 2.3 collective-permute-start.6
  221.9 20.6 %collective-permute-done.7 = f32[64,4,8,136]{3,2,1,0:T(8,128)S(1)} collective-permute-done((f32[64,4,8,136]{3,2,1,0:T(8,128)S(1)}, f32[64,4,8,136]{3,2,1,0:T(8,128)S(1)}, u32[]{:S(2)}, u32[]{:S(2)}) %collective-permute-start.7) | collective-permute-done | bytes 1114144 | tf_op jit(solution)/shard_map/ppermute | solution.py:20
  242.5 4.4 collective-permute-done.6
  246.9 11.0 %pad_maximum_fusion.1 = (f32[64,20,8,136]{3,2,1,0:T(8,128)}, f32[64,20,8,136]{3,2,1,0:T(8,128)}) fusion(f32[64,4,8,136]{3,2,1,0:T(8,128)S(1)} %collective-permute-done.6, f32[64,16,8,4]{3,2,1,0:T(8,128)S(1)} %copy-done.9, f32[64,16,8,128]{3,2,1,0:T(8,128)S(1)} %copy-done, f32[64,16,8,4]{3,2,1,0:T(8,128)S(1)} %copy-done.12, ...), kind=kLoop, calls=%fused_computation.69 | loop fusion | flops 8355840 | bytes 17825792 | tf_op jit(solution)/shard_map/concatenate | solution.py:24
  257.9 12.4 %select_maximum_fusion.8 = f32[64,24,16,136]{3,2,1,0:T(8,128)} fusion(f32[64,4,8,136]{3,2,1,0:T(8,128)S(1)} %collective-permute-done.6, f32[64,4,8,136]{3,2,1,0:T(8,128)S(1)} %collective-permute-done.7, f32[64,16,8,4]{3,2,1,0:T(8,128)S(1)} %copy-done.9, f32[64,16,8,128]{3,2,1,0:T(8,128)S(1)} %copy-done, f32[64,16,8,4]{3,2,1,0:T(8,128)S(1)} %copy-done.12), kind=kLoop, calls=%fused_computation.10 | loop fusion | flops 40108032 | bytes 20054016 | tf_op jit(solution)/shard_map/concatenate | solution.py:24
  270.4 88.6 %fusion.50 = f32[64,16,8,128]{3,2,1,0:T(8,128)} fusion(f32[64,16,8,4]{3,2,1,0:T(8,128)} %copy.95, f32[64,16,8,128]{3,2,1,0:T(8,128)} %fusion.1, f32[64,16,8,4]{3,2,1,0:T(8,128)} %copy.96, f32[64,24,16,136]{3,2,1,0:T(8,128)} %select_maximum_fusion.8, f32[64,20,8,136]{3,2,1,0:T(8,128)} %get-tuple-element.30, f32[64,20,8,136]{3,2,1,0:T(8,128)} %get-tuple-element.29, ...), kind=kLoop, calls=%fused_computation.125 | loop fusion | flops 42991616 | bytes 80019456 | tf_op jit(solution)/shard_map/add | solution.py:72
  359.0 8.2 fusion.135
  367.1 3.7 copy.100
  372.1 3.7 copy.99
  375.8 4.9 collective-permute-start.8
  380.8 4.6 copy.102
  385.4 4.5 copy.101
  389.8 4.7 pad_maximum_fusion.15
  394.5 2.9 collective-permute-start.11
  399.3 21.0 %collective-permute-done.11 = f32[64,4,8,136]{3,2,1,0:T(8,128)S(1)} collective-permute-done((f32[64,4,8,136]{3,2,1,0:T(8,128)S(1)}, f32[64,4,8,136]{3,2,1,0:T(8,128)S(1)}, u32[]{:S(2)}, u32[]{:S(2)}) %collective-permute-start.11) | collective-permute-done | bytes 1114144 | tf_op jit(solution)/shard_map/ppermute | solution.py:20
  420.4 4.4 collective-permute-done.10
  424.8 11.0 %pad_maximum_fusion.2 = (f32[64,20,8,136]{3,2,1,0:T(8,128)}, f32[64,20,8,136]{3,2,1,0:T(8,128)}) fusion(f32[64,4,8,136]{3,2,1,0:T(8,128)S(1)} %collective-permute-done.10, f32[64,16,8,4]{3,2,1,0:T(8,128)S(1)} %copy-done.10, f32[64,16,8,128]{3,2,1,0:T(8,128)S(1)} %copy-done.2, f32[64,16,8,4]{3,2,1,0:T(8,128)S(1)} %copy-done.13, ...), kind=kLoop, calls=%fused_computation.71 | loop fusion | flops 8355840 | bytes 17825792 | tf_op jit(solution)/shard_map/concatenate | solution.py:24
  435.8 12.4 %select_maximum_fusion.4 = f32[64,24,16,136]{3,2,1,0:T(8,128)} fusion(f32[64,4,8,136]{3,2,1,0:T(8,128)S(1)} %collective-permute-done.10, f32[64,4,8,136]{3,2,1,0:T(8,128)S(1)} %collective-permute-done.11, f32[64,16,8,4]{3,2,1,0:T(8,128)S(1)} %copy-done.10, f32[64,16,8,128]{3,2,1,0:T(8,128)S(1)} %copy-done.2, f32[64,16,8,4]{3,2,1,0:T(8,128)S(1)} %copy-done.13), kind=kLoop, calls=%fused_computation.6 | loop fusion | flops 40108032 | bytes 20054016 | tf_op jit(solution)/shard_map/concatenate | solution.py:24
  448.2 89.1 %fusion.29 = f32[64,16,8,128]{3,2,1,0:T(8,128)} fusion(f32[64,16,8,4]{3,2,1,0:T(8,128)} %copy.101, f32[64,16,8,128]{3,2,1,0:T(8,128)} %fusion.50, f32[64,16,8,4]{3,2,1,0:T(8,128)} %copy.102, f32[64,24,16,136]{3,2,1,0:T(8,128)} %select_maximum_fusion.4, f32[64,20,8,136]{3,2,1,0:T(8,128)} %get-tuple-element.26, f32[64,20,8,136]{3,2,1,0:T(8,128)} %get-tuple-element.25, ...), kind=kLoop, calls=%fused_computation.104 | loop fusion | flops 42991616 | bytes 80019456 | tf_op jit(solution)/shard_map/add | solution.py:72
  537.3 8.2 fusion.134
  545.4 3.7 copy.106
  549.1 3.7 copy.105
  552.8 4.1 collective-permute-start.12
  559.0 5.5 collective-permute-done.13
  564.5 4.6 copy.108
  569.0 4.6 copy.107
  573.6 4.7 pad_maximum_fusion.12
  578.3 3.7 collective-permute-start.15
  584.0 4.7 fusion.113
  588.7 4.7 fusion.116
  593.4 4.8 fusion.119
  598.2 6.8 collective-permute-done.15
  605.0 4.7 collective-permute-done.14
  609.7 11.0 %pad_maximum_fusion.3 = (f32[64,20,8,136]{3,2,1,0:T(8,128)}, f32[64,20,8,136]{3,2,1,0:T(8,128)}) fusion(f32[64,4,8,136]{3,2,1,0:T(8,128)S(1)} %collective-permute-done.14, f32[64,16,8,4]{3,2,1,0:T(8,128)S(1)} %copy-done.6, f32[64,16,8,128]{3,2,1,0:T(8,128)S(1)} %copy-done.4, f32[64,16,8,4]{3,2,1,0:T(8,128)S(1)} %copy-done.7, ...), kind=kLoop, calls=%fused_computation.73 | loop fusion | flops 8355840 | bytes 17825792 | tf_op jit(solution)/shard_map/concatenate | solution.py:24
  620.7 12.4 %select_maximum_fusion = f32[64,24,16,136]{3,2,1,0:T(8,128)} fusion(f32[64,4,8,136]{3,2,1,0:T(8,128)S(1)} %collective-permute-done.14, f32[64,4,8,136]{3,2,1,0:T(8,128)S(1)} %collective-permute-done.15, f32[64,16,8,4]{3,2,1,0:T(8,128)S(1)} %copy-done.6, f32[64,16,8,128]{3,2,1,0:T(8,128)S(1)} %copy-done.4, f32[64,16,8,4]{3,2,1,0:T(8,128)S(1)} %copy-done.7), kind=kLoop, calls=%fused_computation.2 | loop fusion | flops 40108032 | bytes 20054016 | tf_op jit(solution)/shard_map/concatenate | solution.py:24
  633.2 89.8 %fusion.8 = f32[64,16,8,128]{3,2,1,0:T(8,128)} fusion(f32[64,16,8,4]{3,2,1,0:T(8,128)} %copy.107, f32[64,16,8,128]{3,2,1,0:T(8,128)} %fusion.29, f32[64,16,8,4]{3,2,1,0:T(8,128)} %copy.108, f32[64,24,16,136]{3,2,1,0:T(8,128)} %select_maximum_fusion, f32[64,20,8,136]{3,2,1,0:T(8,128)} %get-tuple-element.22, f32[64,20,8,136]{3,2,1,0:T(8,128)} %get-tuple-element.21, ...), kind=kLoop, calls=%fused_computation.83 | loop fusion | flops 42991616 | bytes 80019456 | tf_op jit(solution)/shard_map/add | solution.py:72
  723.0 6.7 fusion.122
  730.0 70.9 %psum.7 = f32[64,64]{0,1:T(8,128)S(1)} all-reduce(f32[64,64]{0,1:T(8,128)S(1)} %convolution_bitcast_fusion), channel_id=1, replica_groups=mesh['grp'=4,'slab'=32] {'grp','slab'}, use_global_device_ids=true, to_apply=%region_2.3 | all-reduce | flops 4096 | bytes 32768 | tf_op jit(solution)/shard_map/psum | solution.py:109
  801.0 5.8 cholesky.16
  807.9 5.5 all-to-all-start
  815.4 4.9 custom-call.7
  820.3 2.1 all-to-all-done
  (67 shorter events, 15.5 us)
Async XLA Ops:
  12.5 10.4 %collective-permute-start.1 = (f32[64,16,8,4]{0,2,3,1:T(8,128)S(1)}, f32[64,16,8,4]{0,2,3,1:T(8,128)S(1)}, u32[]{:S(2)}, u32[]{:S(2)}) collective-permute-start(f32[64,16,8,4]{0,2,3,1:T(8,128)S(1)} %copy.123), channel_id=1, source_target_pairs={{32,0},{64,32},{96,64},{33,1},{65,33},{97,65},{34,2},{66,34},{98,6... | collective-permute-start | bytes 393224 | tf_op jit(solution)/shard_map/ppermute | solution.py:23
  17.5 10.0 %collective-permute-start = (f32[64,16,8,4]{0,2,3,1:T(8,128)S(1)}, f32[64,16,8,4]{0,2,3,1:T(8,128)S(1)}, u32[]{:S(2)}, u32[]{:S(2)}) collective-permute-start(f32[64,16,8,4]{0,2,3,1:T(8,128)S(1)} %copy.122), channel_id=1, source_target_pairs={{0,32},{32,64},{64,96},{1,33},{33,65},{65,97},{2,34},{34,66},{66,9... | collective-permute-start | bytes 393224 | tf_op jit(solution)/shard_map/ppermute | solution.py:20
  32.0 36.9 %copy-start.5 = (f32[64,16,8,128]{3,2,1,0:T(8,128)S(1)}, f32[64,16,8,128]{3,2,1,0:T(8,128)}, u32[]{:S(2)}) copy-start(f32[64,16,8,128]{3,2,1,0:T(8,128)} %param.5) | copy-start | bytes 12582916
  32.0 36.9 %copy-start.8 = (f32[64,16,8,4]{3,2,1,0:T(8,128)S(1)}, f32[64,16,8,4]{3,2,1,0:T(8,128)}, u32[]{:S(2)}) copy-start(f32[64,16,8,4]{3,2,1,0:T(8,128)} %copy.90) | copy-start | bytes 393220
  32.0 36.9 %copy-start.11 = (f32[64,16,8,4]{3,2,1,0:T(8,128)S(1)}, f32[64,16,8,4]{3,2,1,0:T(8,128)}, u32[]{:S(2)}) copy-start(f32[64,16,8,4]{3,2,1,0:T(8,128)} %copy.89) | copy-start | bytes 393220
  36.7 27.8 %collective-permute-start.3 = (f32[64,4,8,136]{3,2,1,0:T(8,128)S(1)}, f32[64,4,8,136]{3,2,1,0:T(8,128)S(1)}, u32[]{:S(2)}, u32[]{:S(2)}) collective-permute-start(f32[64,4,8,136]{3,2,1,0:T(8,128)S(1)} %get-tuple-element.35), channel_id=1, source_target_pairs={{0,1},{1,2},{2,3},{3,4},{4,5},{5,6},{6,7},{7,8},{8,9},{9,10},{10,1... | collective-permute-start | bytes 3342344 | tf_op jit(solution)/shard_map/ppermute | solution.py:20
  41.5 27.4 %collective-permute-start.2 = (f32[64,4,8,136]{3,2,1,0:T(8,128)S(1)}, f32[64,4,8,136]{3,2,1,0:T(8,128)S(1)}, u32[]{:S(2)}, u32[]{:S(2)}) collective-permute-start(f32[64,4,8,136]{3,2,1,0:T(8,128)S(1)} %get-tuple-element.36), channel_id=1, source_target_pairs={{1,0},{2,1},{3,2},{4,3},{5,4},{6,5},{7,6},{8,7},{9,8},{10,9},{11,1... | collective-permute-start | bytes 3342344 | tf_op jit(solution)/shard_map/ppermute | solution.py:23
  79.9 12.4 %copy-start.14 = (f32[16,8,128]{2,1,0:T(8,128)S(1)}, f32[16,8,128]{2,1,0:T(8,128)}, u32[]{:S(2)}) copy-start(f32[16,8,128]{2,1,0:T(8,128)} %param.6) | copy-start | bytes 196612
  192.6 9.8 %collective-permute-start.5 = (f32[64,16,8,4]{0,2,3,1:T(8,128)S(1)}, f32[64,16,8,4]{0,2,3,1:T(8,128)S(1)}, u32[]{:S(2)}, u32[]{:S(2)}) collective-permute-start(f32[64,16,8,4]{0,2,3,1:T(8,128)S(1)} %copy.94), channel_id=1, source_target_pairs={{32,0},{64,32},{96,64},{33,1},{65,33},{97,65},{34,2},{66,34},{98,6... | collective-permute-start | bytes 393224 | tf_op jit(solution)/shard_map/ppermute | solution.py:23
  197.6 9.4 %collective-permute-start.4 = (f32[64,16,8,4]{0,2,3,1:T(8,128)S(1)}, f32[64,16,8,4]{0,2,3,1:T(8,128)S(1)}, u32[]{:S(2)}, u32[]{:S(2)}) collective-permute-start(f32[64,16,8,4]{0,2,3,1:T(8,128)S(1)} %copy.93), channel_id=1, source_target_pairs={{0,32},{32,64},{64,96},{1,33},{33,65},{65,97},{2,34},{34,66},{66,9... | collective-permute-start | bytes 393224 | tf_op jit(solution)/shard_map/ppermute | solution.py:20
  211.5 35.5 %copy-start = (f32[64,16,8,128]{3,2,1,0:T(8,128)S(1)}, f32[64,16,8,128]{3,2,1,0:T(8,128)}, u32[]{:S(2)}) copy-start(f32[64,16,8,128]{3,2,1,0:T(8,128)} %fusion.1) | copy-start | bytes 12582916
  211.5 35.5 %copy-start.9 = (f32[64,16,8,4]{3,2,1,0:T(8,128)S(1)}, f32[64,16,8,4]{3,2,1,0:T(8,128)}, u32[]{:S(2)}) copy-start(f32[64,16,8,4]{3,2,1,0:T(8,128)} %copy.96) | copy-start | bytes 393220
  211.5 35.5 %copy-start.12 = (f32[64,16,8,4]{3,2,1,0:T(8,128)S(1)}, f32[64,16,8,4]{3,2,1,0:T(8,128)}, u32[]{:S(2)}) copy-start(f32[64,16,8,4]{3,2,1,0:T(8,128)} %copy.95) | copy-start | bytes 393220
  216.1 26.4 %collective-permute-start.7 = (f32[64,4,8,136]{3,2,1,0:T(8,128)S(1)}, f32[64,4,8,136]{3,2,1,0:T(8,128)S(1)}, u32[]{:S(2)}, u32[]{:S(2)}) collective-permute-start(f32[64,4,8,136]{3,2,1,0:T(8,128)S(1)} %get-tuple-element.31), channel_id=1, source_target_pairs={{0,1},{1,2},{2,3},{3,4},{4,5},{5,6},{6,7},{7,8},{8,9},{9,10},{10,1... | collective-permute-start | bytes 3342344 | tf_op jit(solution)/shard_map/ppermute | solution.py:20
  219.6 27.4 %collective-permute-start.6 = (f32[64,4,8,136]{3,2,1,0:T(8,128)S(1)}, f32[64,4,8,136]{3,2,1,0:T(8,128)S(1)}, u32[]{:S(2)}, u32[]{:S(2)}) collective-permute-start(f32[64,4,8,136]{3,2,1,0:T(8,128)S(1)} %get-tuple-element.32), channel_id=1, source_target_pairs={{1,0},{2,1},{3,2},{4,3},{5,4},{6,5},{7,6},{8,7},{9,8},{10,9},{11,1... | collective-permute-start | bytes 3342344 | tf_op jit(solution)/shard_map/ppermute | solution.py:23
  370.8 9.9 %collective-permute-start.9 = (f32[64,16,8,4]{0,2,3,1:T(8,128)S(1)}, f32[64,16,8,4]{0,2,3,1:T(8,128)S(1)}, u32[]{:S(2)}, u32[]{:S(2)}) collective-permute-start(f32[64,16,8,4]{0,2,3,1:T(8,128)S(1)} %copy.100), channel_id=1, source_target_pairs={{32,0},{64,32},{96,64},{33,1},{65,33},{97,65},{34,2},{66,34},{98,6... | collective-permute-start | bytes 393224 | tf_op jit(solution)/shard_map/ppermute | solution.py:23
  375.8 9.5 %collective-permute-start.8 = (f32[64,16,8,4]{0,2,3,1:T(8,128)S(1)}, f32[64,16,8,4]{0,2,3,1:T(8,128)S(1)}, u32[]{:S(2)}, u32[]{:S(2)}) collective-permute-start(f32[64,16,8,4]{0,2,3,1:T(8,128)S(1)} %copy.99), channel_id=1, source_target_pairs={{0,32},{32,64},{64,96},{1,33},{33,65},{65,97},{2,34},{34,66},{66,9... | collective-permute-start | bytes 393224 | tf_op jit(solution)/shard_map/ppermute | solution.py:20
  389.8 34.9 %copy-start.2 = (f32[64,16,8,128]{3,2,1,0:T(8,128)S(1)}, f32[64,16,8,128]{3,2,1,0:T(8,128)}, u32[]{:S(2)}) copy-start(f32[64,16,8,128]{3,2,1,0:T(8,128)} %fusion.50) | copy-start | bytes 12582916
  389.8 34.9 %copy-start.10 = (f32[64,16,8,4]{3,2,1,0:T(8,128)S(1)}, f32[64,16,8,4]{3,2,1,0:T(8,128)}, u32[]{:S(2)}) copy-start(f32[64,16,8,4]{3,2,1,0:T(8,128)} %copy.102) | copy-start | bytes 393220
  389.8 34.9 %copy-start.13 = (f32[64,16,8,4]{3,2,1,0:T(8,128)S(1)}, f32[64,16,8,4]{3,2,1,0:T(8,128)}, u32[]{:S(2)}) copy-start(f32[64,16,8,4]{3,2,1,0:T(8,128)} %copy.101) | copy-start | bytes 393220
  394.5 25.9 %collective-permute-start.11 = (f32[64,4,8,136]{3,2,1,0:T(8,128)S(1)}, f32[64,4,8,136]{3,2,1,0:T(8,128)S(1)}, u32[]{:S(2)}, u32[]{:S(2)}) collective-permute-start(f32[64,4,8,136]{3,2,1,0:T(8,128)S(1)} %get-tuple-element.27), channel_id=1, source_target_pairs={{0,1},{1,2},{2,3},{3,4},{4,5},{5,6},{6,7},{7,8},{8,9},{9,10},{10,1... | collective-permute-start | bytes 3342344 | tf_op jit(solution)/shard_map/ppermute | solution.py:20
  397.4 27.4 %collective-permute-start.10 = (f32[64,4,8,136]{3,2,1,0:T(8,128)S(1)}, f32[64,4,8,136]{3,2,1,0:T(8,128)S(1)}, u32[]{:S(2)}, u32[]{:S(2)}) collective-permute-start(f32[64,4,8,136]{3,2,1,0:T(8,128)S(1)} %get-tuple-element.28), channel_id=1, source_target_pairs={{1,0},{2,1},{3,2},{4,3},{5,4},{6,5},{7,6},{8,7},{9,8},{10,9},{11,1... | collective-permute-start | bytes 3342344 | tf_op jit(solution)/shard_map/ppermute | solution.py:23
  545.4 13.2 %copy-start.16 = (s32[64,1]{0,1:T(1,128)S(1)}, s32[64,1]{0,1:T(1,128)}, u32[]{:S(2)}) copy-start(s32[64,1]{0,1:T(1,128)} %param.8) | copy-start | bytes 772
  552.8 16.2 %collective-permute-start.12 = (f32[64,16,8,4]{0,2,3,1:T(8,128)S(1)}, f32[64,16,8,4]{0,2,3,1:T(8,128)S(1)}, u32[]{:S(2)}, u32[]{:S(2)}) collective-permute-start(f32[64,16,8,4]{0,2,3,1:T(8,128)S(1)} %copy.105), channel_id=1, source_target_pairs={{0,32},{32,64},{64,96},{1,33},{33,65},{65,97},{2,34},{34,66},{66,9... | collective-permute-start | bytes 393224 | tf_op jit(solution)/shard_map/ppermute | solution.py:20
  557.0 7.5 collective-permute-start.13
  573.6 10.4 %copy-start.1 = (f32[64,16,8,128]{3,2,1,0:T(8,128)S(1)}, f32[64,16,8,128]{3,2,1,0:T(8,128)}, u32[]{:S(2)}) copy-start(f32[64,16,8,128]{3,2,1,0:T(8,128)} %fusion.1) | copy-start | bytes 12582916
  573.6 10.4 %copy-start.15 = (s32[64]{0:T(128)S(1)}, s32[64]{0:T(128)}, u32[]{:S(2)}) copy-start(s32[64]{0:T(128)} %param.7) | copy-start | bytes 772
  573.6 36.1 %copy-start.7 = (f32[64,16,8,4]{3,2,1,0:T(8,128)S(1)}, f32[64,16,8,4]{3,2,1,0:T(8,128)}, u32[]{:S(2)}) copy-start(f32[64,16,8,4]{3,2,1,0:T(8,128)} %copy.107) | copy-start | bytes 393220
  578.3 10.4 %copy-start.3 = (f32[64,16,8,128]{3,2,1,0:T(8,128)S(1)}, f32[64,16,8,128]{3,2,1,0:T(8,128)}, u32[]{:S(2)}) copy-start(f32[64,16,8,128]{3,2,1,0:T(8,128)} %fusion.50) | copy-start | bytes 12582916
  578.3 26.7 %collective-permute-start.15 = (f32[64,4,8,136]{3,2,1,0:T(8,128)S(1)}, f32[64,4,8,136]{3,2,1,0:T(8,128)S(1)}, u32[]{:S(2)}, u32[]{:S(2)}) collective-permute-start(f32[64,4,8,136]{3,2,1,0:T(8,128)S(1)} %get-tuple-element.23), channel_id=1, source_target_pairs={{0,1},{1,2},{2,3},{3,4},{4,5},{5,6},{6,7},{7,8},{8,9},{9,10},{10,1... | collective-permute-start | bytes 3342344 | tf_op jit(solution)/shard_map/ppermute | solution.py:20
  582.0 27.7 %collective-permute-start.14 = (f32[64,4,8,136]{3,2,1,0:T(8,128)S(1)}, f32[64,4,8,136]{3,2,1,0:T(8,128)S(1)}, u32[]{:S(2)}, u32[]{:S(2)}) collective-permute-start(f32[64,4,8,136]{3,2,1,0:T(8,128)S(1)} %get-tuple-element.24), channel_id=1, source_target_pairs={{1,0},{2,1},{3,2},{4,3},{5,4},{6,5},{7,6},{8,7},{9,8},{10,9},{11,1... | collective-permute-start | bytes 3342344 | tf_op jit(solution)/shard_map/ppermute | solution.py:23
  584.0 9.4 %copy-start.4 = (f32[64,16,8,128]{3,2,1,0:T(8,128)S(1)}, f32[64,16,8,128]{3,2,1,0:T(8,128)}, u32[]{:S(2)}) copy-start(f32[64,16,8,128]{3,2,1,0:T(8,128)} %fusion.29) | copy-start | bytes 12582916
  588.7 21.0 %copy-start.6 = (f32[64,16,8,4]{3,2,1,0:T(8,128)S(1)}, f32[64,16,8,4]{3,2,1,0:T(8,128)}, u32[]{:S(2)}) copy-start(f32[64,16,8,4]{3,2,1,0:T(8,128)} %copy.108) | copy-start | bytes 393220
  723.0 6.7 copy-start.17
  807.9 14.5 %all-to-all-start = ((f32[32,8,256]{2,1,0:T(8,128)}), f32[32,8,256]{2,1,0:T(8,128)S(1)}, u32[]{:S(2)}, u32[]{:S(2)}) async-start(f32[32,8,256]{2,1,0:T(8,128)} %fusion.126), calls=%async_computation | async-start | bytes 524288 | tf_op jit(solution)/shard_map/all_to_all | solution.py:101
where the time goes:
time: 832 us; the launch traced here: 825 us
  other arithmetic  481 us (58%)
  local copies, waits for them, and re-layouts  101 us (12%)
  waiting for transfers between devices  95.1 us (11%)
  blocking collectives  70.9 us (9%)
  starting transfers between devices  52.9 us (6%)
  matrix products  22.8 us (3%)
    add x4, other arithmetic, per_device(): advanced = 2.0 * current - previous + speed * laplace(pad_middle(extended))  356 us
    concatenate x12, other arithmetic, with_halo(): block = jnp.concatenate([low, block, high], axis=dim)  112 us
    psum x1, blocking collectives, per_device(): lower = jnp.linalg.cholesky(lax.psum(gram, ('grp', 'slab')))  70.9 us
    ppermute x8, waiting for transfers between devices, with_halo(): lax.ppermute(lax.slice_in_dim(block, block.shape[dim] - width, None, axis...  69.3 us
    slice x7, local copies, waits for them, and re-layouts, with_halo(): lax.slice_in_dim(block, 0, width, axis=dim)  43.7 us
    ppermute x8, starting transfers between devices, with_halo(): lax.ppermute(lax.slice_in_dim(block, block.shape[dim] - width, None, axis...  33.6 us
    ppermute x8, waiting for transfers between devices, with_halo(): lax.ppermute(lax.slice_in_dim(block, 0, width, axis=dim), axis, backward)  23.7 us
    dot_general x4, matrix products, per_device(): jnp.dot(current.reshape(PROBES, cells), picker, preferred_element_type=jn...  20.8 us
  transfers between devices with their start and end apart: 17, of which 11 were waited for; matrix products, arithmetic and copies ran while one was open for 6% of the time, Pallas kernels for 0%

commit v1 on v0

--- a/solution.py
+++ b/solution.py
@@ -106,7 +106,7 @@
         tiled=True,
     )
     incoming = incoming.reshape(n_slab * capacity, STEPS * PROBES)
-    lower = jnp.linalg.cholesky(lax.psum(gram, ("grp", "slab")))
+    lower = jnp.linalg.cholesky(lax.psum(lax.psum(gram, "grp"), "slab"))
     row_count = rec_count * n_slab * n_group * STEPS
     r_factor = lower.T / math.sqrt(row_count)
     solved = jax.scipy.linalg.solve_triangular(

time: 832 us -> 902 us (1.084)
  blocking collectives: 70.9 us -> 132 us
    psum x1 -> x2, blocking collectives: 70.9 us -> 132 us  [per_device(): lower = jnp.linalg.cholesky(lax.psum(lax.psum(gram, 'grp'), 'slab'))]
where the time goes in v1:
time: 902 us; the launch traced here: 895 us
  other arithmetic  486 us (54%)
  blocking collectives  132 us (15%)
  local copies, waits for them, and re-layouts  100 us (11%)
  waiting for transfers between devices  95.1 us (11%)
  starting transfers between devices  57.1 us (6%)
  matrix products  22.8 us (3%)
    add x4, other arithmetic, per_device(): advanced = 2.0 * current - previous + speed * laplace(pad_middle(extended))  361 us
    psum x2, blocking collectives, per_device(): lower = jnp.linalg.cholesky(lax.psum(lax.psum(gram, 'grp'), 'slab'))  132 us
    concatenate x12, other arithmetic, with_halo(): block = jnp.concatenate([low, block, high], axis=dim)  112 us
    ppermute x8, waiting for transfers between devices, with_halo(): lax.ppermute(lax.slice_in_dim(block, block.shape[dim] - width, None, axis...  69.3 us
    slice x7, local copies, waits for them, and re-layouts, with_halo(): lax.slice_in_dim(block, 0, width, axis=dim)  43.8 us
    ppermute x8, starting transfers between devices, with_halo(): lax.ppermute(lax.slice_in_dim(block, block.shape[dim] - width, None, axis...  34.1 us
    ppermute x8, waiting for transfers between devices, with_halo(): lax.ppermute(lax.slice_in_dim(block, 0, width, axis=dim), axis, backward)  23.6 us
    dot_general x4, matrix products, per_device(): jnp.dot(current.reshape(PROBES, cells), picker, preferred_element_type=jn...  20.8 us
  transfers between devices with their start and end apart: 17, of which 11 were waited for; matrix products, arithmetic and copies ran while one was open for 6% of the time, Pallas kernels for 0%

profile of v1, /device:TPU:1, one launch (start us, length us, event | category | flops | bytes accessed | tf_op | source)
XLA Modules:
  0.0 895.1 jit_solution(15041402818365297041)
XLA Ops:
  0.6 8.2 fusion.137
  8.8 3.7 copy.123
  13.8 3.7 copy.122
  17.5 5.0 collective-permute-start
  22.9 4.6 copy.90
  27.4 4.5 copy.89
  31.9 4.7 pad_maximum_fusion.21
  36.6 4.9 collective-permute-start.3
  43.6 20.9 %collective-permute-done.3 = f32[64,4,8,136]{3,2,1,0:T(8,128)S(1)} collective-permute-done((f32[64,4,8,136]{3,2,1,0:T(8,128)S(1)}, f32[64,4,8,136]{3,2,1,0:T(8,128)S(1)}, u32[]{:S(2)}, u32[]{:S(2)}) %collective-permute-start.3) | collective-permute-done | bytes 1114144 | tf_op jit(solution)/shard_map/ppermute | solution.py:20
  64.5 4.4 collective-permute-done.2
  68.9 11.0 %pad_maximum_fusion = (f32[64,20,8,136]{3,2,1,0:T(8,128)}, f32[64,20,8,136]{3,2,1,0:T(8,128)}) fusion(f32[64,4,8,136]{3,2,1,0:T(8,128)S(1)} %collective-permute-done.2, f32[64,16,8,4]{3,2,1,0:T(8,128)S(1)} %copy-done.8, f32[64,16,8,128]{3,2,1,0:T(8,128)S(1)} %copy-done.5, f32[64,16,8,4]{3,2,1,0:T(8,128)S(1)} %copy-done.11, ...), kind=kLoop, calls=%fused_computation.67 | loop fusion | flops 8355840 | bytes 17825792 | tf_op jit(solution)/shard_map/concatenate | solution.py:24
  79.9 12.4 %select_maximum_fusion.12 = f32[64,24,16,136]{3,2,1,0:T(8,128)} fusion(f32[64,4,8,136]{3,2,1,0:T(8,128)S(1)} %collective-permute-done.2, f32[64,4,8,136]{3,2,1,0:T(8,128)S(1)} %collective-permute-done.3, f32[64,16,8,4]{3,2,1,0:T(8,128)S(1)} %copy-done.8, f32[64,16,8,128]{3,2,1,0:T(8,128)S(1)} %copy-done.5, f32[64,16,8,4]{3,2,1,0:T(8,128)S(1)} %copy-done.11), kind=kLoop, calls=%fused_computation.14 | loop fusion | flops 40108032 | bytes 20054016 | tf_op jit(solution)/shard_map/concatenate | solution.py:24
  92.3 88.5 %fusion.1 = f32[64,16,8,128]{3,2,1,0:T(8,128)} fusion(f32[64,16,8,128]{3,2,1,0:T(8,128)} %param.5, f32[64,16,8,4]{3,2,1,0:T(8,128)} %copy.89, f32[64,16,8,4]{3,2,1,0:T(8,128)} %copy.90, f32[64,24,16,136]{3,2,1,0:T(8,128)} %select_maximum_fusion.12, f32[64,20,8,136]{3,2,1,0:T(8,128)} %get-tuple-element.34, f32[64,20,8,136]{3,2,1,0:T(8,128)} %get-tuple-element.33, ...), kind=kLoop, calls=%fused_computation.76 | loop fusion | flops 42991616 | bytes 75825152 | tf_op jit(solution)/shard_map/add | solution.py:72
  180.8 8.2 fusion.136
  188.9 3.7 copy.94
  193.9 3.7 copy.93
  197.6 4.7 collective-permute-start.4
  202.4 4.5 copy.96
  206.9 4.5 copy.95
  211.4 4.7 pad_maximum_fusion.18
  216.1 3.5 collective-permute-start.7
  219.6 2.3 collective-permute-start.6
  221.9 20.6 %collective-permute-done.7 = f32[64,4,8,136]{3,2,1,0:T(8,128)S(1)} collective-permute-done((f32[64,4,8,136]{3,2,1,0:T(8,128)S(1)}, f32[64,4,8,136]{3,2,1,0:T(8,128)S(1)}, u32[]{:S(2)}, u32[]{:S(2)}) %collective-permute-start.7) | collective-permute-done | bytes 1114144 | tf_op jit(solution)/shard_map/ppermute | solution.py:20
  242.6 4.4 collective-permute-done.6
  247.0 11.0 %pad_maximum_fusion.1 = (f32[64,20,8,136]{3,2,1,0:T(8,128)}, f32[64,20,8,136]{3,2,1,0:T(8,128)}) fusion(f32[64,4,8,136]{3,2,1,0:T(8,128)S(1)} %collective-permute-done.6, f32[64,16,8,4]{3,2,1,0:T(8,128)S(1)} %copy-done.9, f32[64,16,8,128]{3,2,1,0:T(8,128)S(1)} %copy-done, f32[64,16,8,4]{3,2,1,0:T(8,128)S(1)} %copy-done.12, ...), kind=kLoop, calls=%fused_computation.69 | loop fusion | flops 8355840 | bytes 17825792 | tf_op jit(solution)/shard_map/concatenate | solution.py:24
  258.0 12.4 %select_maximum_fusion.8 = f32[64,24,16,136]{3,2,1,0:T(8,128)} fusion(f32[64,4,8,136]{3,2,1,0:T(8,128)S(1)} %collective-permute-done.6, f32[64,4,8,136]{3,2,1,0:T(8,128)S(1)} %collective-permute-done.7, f32[64,16,8,4]{3,2,1,0:T(8,128)S(1)} %copy-done.9, f32[64,16,8,128]{3,2,1,0:T(8,128)S(1)} %copy-done, f32[64,16,8,4]{3,2,1,0:T(8,128)S(1)} %copy-done.12), kind=kLoop, calls=%fused_computation.10 | loop fusion | flops 40108032 | bytes 20054016 | tf_op jit(solution)/shard_map/concatenate | solution.py:24
  270.4 90.5 %fusion.50 = f32[64,16,8,128]{3,2,1,0:T(8,128)} fusion(f32[64,16,8,4]{3,2,1,0:T(8,128)} %copy.95, f32[64,16,8,128]{3,2,1,0:T(8,128)} %fusion.1, f32[64,16,8,4]{3,2,1,0:T(8,128)} %copy.96, f32[64,24,16,136]{3,2,1,0:T(8,128)} %select_maximum_fusion.8, f32[64,20,8,136]{3,2,1,0:T(8,128)} %get-tuple-element.30, f32[64,20,8,136]{3,2,1,0:T(8,128)} %get-tuple-element.29, ...), kind=kLoop, calls=%fused_computation.125 | loop fusion | flops 42991616 | bytes 80019456 | tf_op jit(solution)/shard_map/add | solution.py:72
  360.9 8.2 fusion.135
  369.2 3.7 copy.100
  374.1 3.7 copy.99
  377.9 4.9 collective-permute-start.8
  382.8 4.5 copy.102
  387.3 4.5 copy.101
  391.8 4.7 pad_maximum_fusion.15
  396.4 3.0 collective-permute-start.11
  401.4 21.0 %collective-permute-done.11 = f32[64,4,8,136]{3,2,1,0:T(8,128)S(1)} collective-permute-done((f32[64,4,8,136]{3,2,1,0:T(8,128)S(1)}, f32[64,4,8,136]{3,2,1,0:T(8,128)S(1)}, u32[]{:S(2)}, u32[]{:S(2)}) %collective-permute-start.11) | collective-permute-done | bytes 1114144 | tf_op jit(solution)/shard_map/ppermute | solution.py:20
  422.4 4.4 collective-permute-done.10
  426.8 11.0 %pad_maximum_fusion.2 = (f32[64,20,8,136]{3,2,1,0:T(8,128)}, f32[64,20,8,136]{3,2,1,0:T(8,128)}) fusion(f32[64,4,8,136]{3,2,1,0:T(8,128)S(1)} %collective-permute-done.10, f32[64,16,8,4]{3,2,1,0:T(8,128)S(1)} %copy-done.10, f32[64,16,8,128]{3,2,1,0:T(8,128)S(1)} %copy-done.2, f32[64,16,8,4]{3,2,1,0:T(8,128)S(1)} %copy-done.13, ...), kind=kLoop, calls=%fused_computation.71 | loop fusion | flops 8355840 | bytes 17825792 | tf_op jit(solution)/shard_map/concatenate | solution.py:24
  437.8 12.4 %select_maximum_fusion.4 = f32[64,24,16,136]{3,2,1,0:T(8,128)} fusion(f32[64,4,8,136]{3,2,1,0:T(8,128)S(1)} %collective-permute-done.10, f32[64,4,8,136]{3,2,1,0:T(8,128)S(1)} %collective-permute-done.11, f32[64,16,8,4]{3,2,1,0:T(8,128)S(1)} %copy-done.10, f32[64,16,8,128]{3,2,1,0:T(8,128)S(1)} %copy-done.2, f32[64,16,8,4]{3,2,1,0:T(8,128)S(1)} %copy-done.13), kind=kLoop, calls=%fused_computation.6 | loop fusion | flops 40108032 | bytes 20054016 | tf_op jit(solution)/shard_map/concatenate | solution.py:24
  450.3 90.3 %fusion.29 = f32[64,16,8,128]{3,2,1,0:T(8,128)} fusion(f32[64,16,8,4]{3,2,1,0:T(8,128)} %copy.101, f32[64,16,8,128]{3,2,1,0:T(8,128)} %fusion.50, f32[64,16,8,4]{3,2,1,0:T(8,128)} %copy.102, f32[64,24,16,136]{3,2,1,0:T(8,128)} %select_maximum_fusion.4, f32[64,20,8,136]{3,2,1,0:T(8,128)} %get-tuple-element.26, f32[64,20,8,136]{3,2,1,0:T(8,128)} %get-tuple-element.25, ...), kind=kLoop, calls=%fused_computation.104 | loop fusion | flops 42991616 | bytes 80019456 | tf_op jit(solution)/shard_map/add | solution.py:72
  540.6 8.2 fusion.134
  548.7 3.7 copy.106
  552.4 3.7 copy.105
  556.1 4.1 collective-permute-start.12
  562.3 5.5 collective-permute-done.13
  567.8 4.5 copy.108
  572.3 4.5 copy.107
  576.8 4.7 pad_maximum_fusion.12
  581.4 3.8 collective-permute-start.15
  587.3 4.7 fusion.113
  591.9 4.7 fusion.116
  596.6 4.8 fusion.119
  601.4 6.8 collective-permute-done.15
  608.2 4.6 collective-permute-done.14
  612.9 11.0 %pad_maximum_fusion.3 = (f32[64,20,8,136]{3,2,1,0:T(8,128)}, f32[64,20,8,136]{3,2,1,0:T(8,128)}) fusion(f32[64,4,8,136]{3,2,1,0:T(8,128)S(1)} %collective-permute-done.14, f32[64,16,8,4]{3,2,1,0:T(8,128)S(1)} %copy-done.6, f32[64,16,8,128]{3,2,1,0:T(8,128)S(1)} %copy-done.4, f32[64,16,8,4]{3,2,1,0:T(8,128)S(1)} %copy-done.7, ...), kind=kLoop, calls=%fused_computation.73 | loop fusion | flops 8355840 | bytes 17825792 | tf_op jit(solution)/shard_map/concatenate | solution.py:24
  623.9 12.4 %select_maximum_fusion = f32[64,24,16,136]{3,2,1,0:T(8,128)} fusion(f32[64,4,8,136]{3,2,1,0:T(8,128)S(1)} %collective-permute-done.14, f32[64,4,8,136]{3,2,1,0:T(8,128)S(1)} %collective-permute-done.15, f32[64,16,8,4]{3,2,1,0:T(8,128)S(1)} %copy-done.6, f32[64,16,8,128]{3,2,1,0:T(8,128)S(1)} %copy-done.4, f32[64,16,8,4]{3,2,1,0:T(8,128)S(1)} %copy-done.7), kind=kLoop, calls=%fused_computation.2 | loop fusion | flops 40108032 | bytes 20054016 | tf_op jit(solution)/shard_map/concatenate | solution.py:24
  636.3 92.0 %fusion.8 = f32[64,16,8,128]{3,2,1,0:T(8,128)} fusion(f32[64,16,8,4]{3,2,1,0:T(8,128)} %copy.107, f32[64,16,8,128]{3,2,1,0:T(8,128)} %fusion.29, f32[64,16,8,4]{3,2,1,0:T(8,128)} %copy.108, f32[64,24,16,136]{3,2,1,0:T(8,128)} %select_maximum_fusion, f32[64,20,8,136]{3,2,1,0:T(8,128)} %get-tuple-element.22, f32[64,20,8,136]{3,2,1,0:T(8,128)} %get-tuple-element.21, ...), kind=kLoop, calls=%fused_computation.83 | loop fusion | flops 42991616 | bytes 80019456 | tf_op jit(solution)/shard_map/add | solution.py:72
  728.3 6.7 fusion.122
  735.3 13.8 %psum.14 = f32[64,64]{0,1:T(8,128)S(1)} all-reduce(f32[64,64]{0,1:T(8,128)S(1)} %convolution_bitcast_fusion), channel_id=1, replica_groups=mesh['grp'=4,'slab'=32] {'grp'}, use_global_device_ids=true, to_apply=%region_2.3 | all-reduce | flops 4096 | bytes 32768 | tf_op jit(solution)/shard_map/psum | solution.py:109
  749.1 118.6 %psum.15 = f32[64,64]{0,1:T(8,128)S(1)} all-reduce(f32[64,64]{0,1:T(8,128)S(1)} %psum.14), channel_id=1, replica_groups=mesh['grp'=4,'slab'=32] {'slab'}, use_global_device_ids=true, to_apply=%region_3.4 | all-reduce | flops 4096 | bytes 32768 | tf_op jit(solution)/shard_map/psum | solution.py:109
  867.8 5.8 cholesky.16
  874.7 9.2 %all-to-all-start = ((f32[32,8,256]{2,1,0:T(8,128)}), f32[32,8,256]{2,1,0:T(8,128)S(1)}, u32[]{:S(2)}, u32[]{:S(2)}) async-start(f32[32,8,256]{2,1,0:T(8,128)} %fusion.126), calls=%async_computation | async-start | bytes 524288 | tf_op jit(solution)/shard_map/all_to_all | solution.py:101
  885.8 4.9 custom-call.7
  890.7 2.2 all-to-all-done
  (68 shorter events, 17.6 us)
Async XLA Ops:
  12.5 10.4 %collective-permute-start.1 = (f32[64,16,8,4]{0,2,3,1:T(8,128)S(1)}, f32[64,16,8,4]{0,2,3,1:T(8,128)S(1)}, u32[]{:S(2)}, u32[]{:S(2)}) collective-permute-start(f32[64,16,8,4]{0,2,3,1:T(8,128)S(1)} %copy.123), channel_id=1, source_target_pairs={{32,0},{64,32},{96,64},{33,1},{65,33},{97,65},{34,2},{66,34},{98,6... | collective-permute-start | bytes 393224 | tf_op jit(solution)/shard_map/ppermute | solution.py:23
  17.5 9.9 %collective-permute-start = (f32[64,16,8,4]{0,2,3,1:T(8,128)S(1)}, f32[64,16,8,4]{0,2,3,1:T(8,128)S(1)}, u32[]{:S(2)}, u32[]{:S(2)}) collective-permute-start(f32[64,16,8,4]{0,2,3,1:T(8,128)S(1)} %copy.122), channel_id=1, source_target_pairs={{0,32},{32,64},{64,96},{1,33},{33,65},{65,97},{2,34},{34,66},{66,9... | collective-permute-start | bytes 393224 | tf_op jit(solution)/shard_map/ppermute | solution.py:20
  31.9 37.0 %copy-start.5 = (f32[64,16,8,128]{3,2,1,0:T(8,128)S(1)}, f32[64,16,8,128]{3,2,1,0:T(8,128)}, u32[]{:S(2)}) copy-start(f32[64,16,8,128]{3,2,1,0:T(8,128)} %param.5) | copy-start | bytes 12582916
  31.9 37.0 %copy-start.8 = (f32[64,16,8,4]{3,2,1,0:T(8,128)S(1)}, f32[64,16,8,4]{3,2,1,0:T(8,128)}, u32[]{:S(2)}) copy-start(f32[64,16,8,4]{3,2,1,0:T(8,128)} %copy.90) | copy-start | bytes 393220
  31.9 37.0 %copy-start.11 = (f32[64,16,8,4]{3,2,1,0:T(8,128)S(1)}, f32[64,16,8,4]{3,2,1,0:T(8,128)}, u32[]{:S(2)}) copy-start(f32[64,16,8,4]{3,2,1,0:T(8,128)} %copy.89) | copy-start | bytes 393220
  36.6 27.9 %collective-permute-start.3 = (f32[64,4,8,136]{3,2,1,0:T(8,128)S(1)}, f32[64,4,8,136]{3,2,1,0:T(8,128)S(1)}, u32[]{:S(2)}, u32[]{:S(2)}) collective-permute-start(f32[64,4,8,136]{3,2,1,0:T(8,128)S(1)} %get-tuple-element.35), channel_id=1, source_target_pairs={{0,1},{1,2},{2,3},{3,4},{4,5},{5,6},{6,7},{7,8},{8,9},{9,10},{10,1... | collective-permute-start | bytes 3342344 | tf_op jit(solution)/shard_map/ppermute | solution.py:20
  41.5 27.4 %collective-permute-start.2 = (f32[64,4,8,136]{3,2,1,0:T(8,128)S(1)}, f32[64,4,8,136]{3,2,1,0:T(8,128)S(1)}, u32[]{:S(2)}, u32[]{:S(2)}) collective-permute-start(f32[64,4,8,136]{3,2,1,0:T(8,128)S(1)} %get-tuple-element.36), channel_id=1, source_target_pairs={{1,0},{2,1},{3,2},{4,3},{5,4},{6,5},{7,6},{8,7},{9,8},{10,9},{11,1... | collective-permute-start | bytes 3342344 | tf_op jit(solution)/shard_map/ppermute | solution.py:23
  79.9 12.4 %copy-start.14 = (f32[16,8,128]{2,1,0:T(8,128)S(1)}, f32[16,8,128]{2,1,0:T(8,128)}, u32[]{:S(2)}) copy-start(f32[16,8,128]{2,1,0:T(8,128)} %param.6) | copy-start | bytes 196612
  192.6 9.8 %collective-permute-start.5 = (f32[64,16,8,4]{0,2,3,1:T(8,128)S(1)}, f32[64,16,8,4]{0,2,3,1:T(8,128)S(1)}, u32[]{:S(2)}, u32[]{:S(2)}) collective-permute-start(f32[64,16,8,4]{0,2,3,1:T(8,128)S(1)} %copy.94), channel_id=1, source_target_pairs={{32,0},{64,32},{96,64},{33,1},{65,33},{97,65},{34,2},{66,34},{98,6... | collective-permute-start | bytes 393224 | tf_op jit(solution)/shard_map/ppermute | solution.py:23
  197.6 9.3 %collective-permute-start.4 = (f32[64,16,8,4]{0,2,3,1:T(8,128)S(1)}, f32[64,16,8,4]{0,2,3,1:T(8,128)S(1)}, u32[]{:S(2)}, u32[]{:S(2)}) collective-permute-start(f32[64,16,8,4]{0,2,3,1:T(8,128)S(1)} %copy.93), channel_id=1, source_target_pairs={{0,32},{32,64},{64,96},{1,33},{33,65},{65,97},{2,34},{34,66},{66,9... | collective-permute-start | bytes 393224 | tf_op jit(solution)/shard_map/ppermute | solution.py:20
  211.4 35.6 %copy-start = (f32[64,16,8,128]{3,2,1,0:T(8,128)S(1)}, f32[64,16,8,128]{3,2,1,0:T(8,128)}, u32[]{:S(2)}) copy-start(f32[64,16,8,128]{3,2,1,0:T(8,128)} %fusion.1) | copy-start | bytes 12582916
  211.4 35.6 %copy-start.9 = (f32[64,16,8,4]{3,2,1,0:T(8,128)S(1)}, f32[64,16,8,4]{3,2,1,0:T(8,128)}, u32[]{:S(2)}) copy-start(f32[64,16,8,4]{3,2,1,0:T(8,128)} %copy.96) | copy-start | bytes 393220
  211.4 35.6 %copy-start.12 = (f32[64,16,8,4]{3,2,1,0:T(8,128)S(1)}, f32[64,16,8,4]{3,2,1,0:T(8,128)}, u32[]{:S(2)}) copy-start(f32[64,16,8,4]{3,2,1,0:T(8,128)} %copy.95) | copy-start | bytes 393220
  216.1 26.5 %collective-permute-start.7 = (f32[64,4,8,136]{3,2,1,0:T(8,128)S(1)}, f32[64,4,8,136]{3,2,1,0:T(8,128)S(1)}, u32[]{:S(2)}, u32[]{:S(2)}) collective-permute-start(f32[64,4,8,136]{3,2,1,0:T(8,128)S(1)} %get-tuple-element.31), channel_id=1, source_target_pairs={{0,1},{1,2},{2,3},{3,4},{4,5},{5,6},{6,7},{7,8},{8,9},{9,10},{10,1... | collective-permute-start | bytes 3342344 | tf_op jit(solution)/shard_map/ppermute | solution.py:20
  219.6 27.4 %collective-permute-start.6 = (f32[64,4,8,136]{3,2,1,0:T(8,128)S(1)}, f32[64,4,8,136]{3,2,1,0:T(8,128)S(1)}, u32[]{:S(2)}, u32[]{:S(2)}) collective-permute-start(f32[64,4,8,136]{3,2,1,0:T(8,128)S(1)} %get-tuple-element.32), channel_id=1, source_target_pairs={{1,0},{2,1},{3,2},{4,3},{5,4},{6,5},{7,6},{8,7},{9,8},{10,9},{11,1... | collective-permute-start | bytes 3342344 | tf_op jit(solution)/shard_map/ppermute | solution.py:23
  372.9 9.9 %collective-permute-start.9 = (f32[64,16,8,4]{0,2,3,1:T(8,128)S(1)}, f32[64,16,8,4]{0,2,3,1:T(8,128)S(1)}, u32[]{:S(2)}, u32[]{:S(2)}) collective-permute-start(f32[64,16,8,4]{0,2,3,1:T(8,128)S(1)} %copy.100), channel_id=1, source_target_pairs={{32,0},{64,32},{96,64},{33,1},{65,33},{97,65},{34,2},{66,34},{98,6... | collective-permute-start | bytes 393224 | tf_op jit(solution)/shard_map/ppermute | solution.py:23
  377.9 9.4 %collective-permute-start.8 = (f32[64,16,8,4]{0,2,3,1:T(8,128)S(1)}, f32[64,16,8,4]{0,2,3,1:T(8,128)S(1)}, u32[]{:S(2)}, u32[]{:S(2)}) collective-permute-start(f32[64,16,8,4]{0,2,3,1:T(8,128)S(1)} %copy.99), channel_id=1, source_target_pairs={{0,32},{32,64},{64,96},{1,33},{33,65},{65,97},{2,34},{34,66},{66,9... | collective-permute-start | bytes 393224 | tf_op jit(solution)/shard_map/ppermute | solution.py:20
  391.8 35.0 %copy-start.2 = (f32[64,16,8,128]{3,2,1,0:T(8,128)S(1)}, f32[64,16,8,128]{3,2,1,0:T(8,128)}, u32[]{:S(2)}) copy-start(f32[64,16,8,128]{3,2,1,0:T(8,128)} %fusion.50) | copy-start | bytes 12582916
  391.8 35.0 %copy-start.10 = (f32[64,16,8,4]{3,2,1,0:T(8,128)S(1)}, f32[64,16,8,4]{3,2,1,0:T(8,128)}, u32[]{:S(2)}) copy-start(f32[64,16,8,4]{3,2,1,0:T(8,128)} %copy.102) | copy-start | bytes 393220
  391.8 35.0 %copy-start.13 = (f32[64,16,8,4]{3,2,1,0:T(8,128)S(1)}, f32[64,16,8,4]{3,2,1,0:T(8,128)}, u32[]{:S(2)}) copy-start(f32[64,16,8,4]{3,2,1,0:T(8,128)} %copy.101) | copy-start | bytes 393220
  396.4 26.0 %collective-permute-start.11 = (f32[64,4,8,136]{3,2,1,0:T(8,128)S(1)}, f32[64,4,8,136]{3,2,1,0:T(8,128)S(1)}, u32[]{:S(2)}, u32[]{:S(2)}) collective-permute-start(f32[64,4,8,136]{3,2,1,0:T(8,128)S(1)} %get-tuple-element.27), channel_id=1, source_target_pairs={{0,1},{1,2},{2,3},{3,4},{4,5},{5,6},{6,7},{7,8},{8,9},{9,10},{10,1... | collective-permute-start | bytes 3342344 | tf_op jit(solution)/shard_map/ppermute | solution.py:20
  399.4 27.4 %collective-permute-start.10 = (f32[64,4,8,136]{3,2,1,0:T(8,128)S(1)}, f32[64,4,8,136]{3,2,1,0:T(8,128)S(1)}, u32[]{:S(2)}, u32[]{:S(2)}) collective-permute-start(f32[64,4,8,136]{3,2,1,0:T(8,128)S(1)} %get-tuple-element.28), channel_id=1, source_target_pairs={{1,0},{2,1},{3,2},{4,3},{5,4},{6,5},{7,6},{8,7},{9,8},{10,9},{11,1... | collective-permute-start | bytes 3342344 | tf_op jit(solution)/shard_map/ppermute | solution.py:23
  548.7 13.2 %copy-start.16 = (s32[64,1]{0,1:T(1,128)S(1)}, s32[64,1]{0,1:T(1,128)}, u32[]{:S(2)}) copy-start(s32[64,1]{0,1:T(1,128)} %param.8) | copy-start | bytes 772
  556.1 16.1 %collective-permute-start.12 = (f32[64,16,8,4]{0,2,3,1:T(8,128)S(1)}, f32[64,16,8,4]{0,2,3,1:T(8,128)S(1)}, u32[]{:S(2)}, u32[]{:S(2)}) collective-permute-start(f32[64,16,8,4]{0,2,3,1:T(8,128)S(1)} %copy.105), channel_id=1, source_target_pairs={{0,32},{32,64},{64,96},{1,33},{33,65},{65,97},{2,34},{34,66},{66,9... | collective-permute-start | bytes 393224 | tf_op jit(solution)/shard_map/ppermute | solution.py:20
  560.3 7.5 collective-permute-start.13
  576.7 10.5 %copy-start.1 = (f32[64,16,8,128]{3,2,1,0:T(8,128)S(1)}, f32[64,16,8,128]{3,2,1,0:T(8,128)}, u32[]{:S(2)}) copy-start(f32[64,16,8,128]{3,2,1,0:T(8,128)} %fusion.1) | copy-start | bytes 12582916
  576.7 10.5 %copy-start.15 = (s32[64]{0:T(128)S(1)}, s32[64]{0:T(128)}, u32[]{:S(2)}) copy-start(s32[64]{0:T(128)} %param.7) | copy-start | bytes 772
  576.7 36.1 %copy-start.7 = (f32[64,16,8,4]{3,2,1,0:T(8,128)S(1)}, f32[64,16,8,4]{3,2,1,0:T(8,128)}, u32[]{:S(2)}) copy-start(f32[64,16,8,4]{3,2,1,0:T(8,128)} %copy.107) | copy-start | bytes 393220
  581.4 10.5 %copy-start.3 = (f32[64,16,8,128]{3,2,1,0:T(8,128)S(1)}, f32[64,16,8,128]{3,2,1,0:T(8,128)}, u32[]{:S(2)}) copy-start(f32[64,16,8,128]{3,2,1,0:T(8,128)} %fusion.50) | copy-start | bytes 12582916
  581.4 26.8 %collective-permute-start.15 = (f32[64,4,8,136]{3,2,1,0:T(8,128)S(1)}, f32[64,4,8,136]{3,2,1,0:T(8,128)S(1)}, u32[]{:S(2)}, u32[]{:S(2)}) collective-permute-start(f32[64,4,8,136]{3,2,1,0:T(8,128)S(1)} %get-tuple-element.23), channel_id=1, source_target_pairs={{0,1},{1,2},{2,3},{3,4},{4,5},{5,6},{6,7},{7,8},{8,9},{9,10},{10,1... | collective-permute-start | bytes 3342344 | tf_op jit(solution)/shard_map/ppermute | solution.py:20
  585.3 27.6 %collective-permute-start.14 = (f32[64,4,8,136]{3,2,1,0:T(8,128)S(1)}, f32[64,4,8,136]{3,2,1,0:T(8,128)S(1)}, u32[]{:S(2)}, u32[]{:S(2)}) collective-permute-start(f32[64,4,8,136]{3,2,1,0:T(8,128)S(1)} %get-tuple-element.24), channel_id=1, source_target_pairs={{1,0},{2,1},{3,2},{4,3},{5,4},{6,5},{7,6},{8,7},{9,8},{10,9},{11,1... | collective-permute-start | bytes 3342344 | tf_op jit(solution)/shard_map/ppermute | solution.py:23
  587.3 9.3 %copy-start.4 = (f32[64,16,8,128]{3,2,1,0:T(8,128)S(1)}, f32[64,16,8,128]{3,2,1,0:T(8,128)}, u32[]{:S(2)}) copy-start(f32[64,16,8,128]{3,2,1,0:T(8,128)} %fusion.29) | copy-start | bytes 12582916
  591.9 20.9 %copy-start.6 = (f32[64,16,8,4]{3,2,1,0:T(8,128)S(1)}, f32[64,16,8,4]{3,2,1,0:T(8,128)}, u32[]{:S(2)}) copy-start(f32[64,16,8,4]{3,2,1,0:T(8,128)} %copy.108) | copy-start | bytes 393220
  728.3 6.7 copy-start.17
  874.7 18.3 %all-to-all-start = ((f32[32,8,256]{2,1,0:T(8,128)}), f32[32,8,256]{2,1,0:T(8,128)S(1)}, u32[]{:S(2)}, u32[]{:S(2)}) async-start(f32[32,8,256]{2,1,0:T(8,128)} %fusion.126), calls=%async_computation | async-start | bytes 524288 | tf_op jit(solution)/shard_map/all_to_all | solution.py:101
